TPU v7x, 256 devices: a whole 4x4x8 slice. The times are simulated.
256 devices in a mesh: aux: 32 (over y, x, core), orb: 8 (over z).
Axes of the slice: x: 4, y: 4, z: 8, core: 2. Of those that a mesh axis runs over, the one named last changes fastest.
Arguments:
- band_pattern: int32 [256, 8], P('aux'), may hold values 0 or 1
- density_in: bfloat16 [256, 8, 128, 128], P('aux', 'orb')
- field_terms: bfloat16 [2, 256, 8, 128, 128], P(None, 'aux', 'orb'), may hold values from -3 to 3
- fit_blocks: int32 [1], replicated, may hold values from 0 to 255
- tensor: bfloat16 [1, 3072, 8, 16384], P(None, 'aux', 'orb'), may hold values from -0.015625 to 0.015625
- metric_inv: float32 [1, 3072, 3072], P(None, 'aux')
Outputs:
- response: bfloat16 [2, 256, 8, 128, 128], P(None, 'aux', 'orb')
- coefficients: float32 [1, 2, 3072], P(None, None, 'aux')
All inputs are finite; a program needn't handle non-finite values. No bound on the sum of `band_pattern` on one device may be relied on, other than what follows from the above.
Results may differ from a plain program's by a relative error of at most 0.0055.
Values may be sent and summed in bfloat16 or wider, within the bound.
A program may use at most 192 MiB of HBM per device.

v0:
```python
import jax
import jax.numpy as jnp
from jax import lax
from jax.sharding import PartitionSpec as P


def padded_2(block, sides, width):
    for axis, dim in sides:
        count = lax.axis_size(axis)
        forward = [(i, i + 1) for i in range(count - 1)]
        backward = [(target, source) for source, target in forward]
        low = lax.ppermute(
            lax.slice_in_dim(block, block.shape[dim] - width, None, axis=dim), axis, forward
        )
        high = lax.ppermute(lax.slice_in_dim(block, 0, width, axis=dim), axis, backward)
        block = jnp.concatenate([low, block, high], axis=dim)
    return block


def sent_to_all(x, axis):
    copies = jnp.broadcast_to(x, (lax.axis_size(axis), *x.shape))
    return lax.all_to_all(copies, axis, split_axis=0, concat_axis=0, tiled=True)


def over_copies(x, axis):
    everything = sent_to_all(x, axis)
    return jnp.sum(everything.astype(jnp.float32), axis=0)


def over_copies_2(x, axis):
    everything = sent_to_all(x, axis)
    return jnp.sum(everything, axis=0)


def joined_along(pieces, dim):
    pieces = jnp.moveaxis(pieces, 0, dim)
    lengths = pieces.shape
    return pieces.reshape(*lengths[:dim], lengths[dim] * lengths[dim + 1], *lengths[dim + 2 :])


def gathered_copies(x, axis, dim):
    pieces = sent_to_all(x, axis)
    return joined_along(pieces, dim)


def slide_slots(blocks, offset):
    slot_count = blocks.shape[2]
    if offset >= 0:
        padded = jnp.pad(blocks, ((0, 0), (0, 0), (offset, 0), (0, 0), (0, 0)))
        return padded[:, :, :slot_count]
    padded = jnp.pad(blocks, ((0, 0), (0, 0), (0, -offset), (0, 0), (0, 0)))
    return padded[:, :, -offset : -offset + slot_count]


def band_keep(band_pattern, first_row, total_rows):
    slot_count = band_pattern.shape[1]
    half_band = slot_count // 2
    row_ids = first_row + jnp.arange(band_pattern.shape[0], dtype=jnp.int32)[:, None]
    columns = row_ids + jnp.arange(slot_count, dtype=jnp.int32)[None, :] - half_band
    return (band_pattern == 1) & (columns >= 0) & (columns < total_rows)


def own_slot_product(factor_left, right_rims, my_slot):
    count_rows = factor_left.shape[1]
    slot_count = factor_left.shape[2]
    half_band = slot_count // 2
    lead_count = right_rims.shape[0]
    total = None
    for stride in range(slot_count):
        source_slot = my_slot - stride + half_band
        inside = (source_slot >= 0) & (source_slot < slot_count)
        starts = (
            jnp.int32(0),
            jnp.int32(stride),
            jnp.clip(source_slot, 0, slot_count - 1),
            jnp.int32(0),
            jnp.int32(0),
        )
        sizes = (lead_count, count_rows, 1, right_rims.shape[3], right_rims.shape[4])
        picked = lax.dynamic_slice(right_rims, starts, sizes)[:, :, 0]
        picked = jnp.where(inside, picked, jnp.zeros((), picked.dtype))
        product = jnp.matmul(factor_left[:, :, stride], picked, preferred_element_type=jnp.float32)
        total = product if total is None else total + product
    return total


def all_slot_product(factor_left, right_rims):
    count_rows = factor_left.shape[1]
    slot_count = factor_left.shape[2]
    half_band = slot_count // 2
    total = None
    for stride in range(slot_count):
        source = slide_slots(right_rims[:, stride : stride + count_rows], stride - half_band)
        product = jnp.matmul(
            factor_left[:, :, stride : stride + 1], source, preferred_element_type=jnp.float32
        )
        total = product if total is None else total + product
    return total


def rim_fields(field_rows, half_band):
    return padded_2(field_rows, (("aux", 1),), half_band)


def on_device(band_pattern, density_in, field_terms, fit_blocks, tensor, metric_inv):
    count_rows = density_in.shape[0]
    slot_count = lax.axis_size("orb")
    half_band = slot_count // 2
    total_rows = count_rows * lax.axis_size("aux")
    first_row = lax.axis_index("aux") * count_rows
    my_slot = lax.axis_index("orb")
    keep_all = band_keep(band_pattern, first_row, total_rows)
    keep_own = lax.dynamic_index_in_dim(keep_all, my_slot, 1, keepdims=True)[None, :, :, None, None]
    keep_out = keep_own[:, :, 0]
    zero_half = jnp.zeros((), jnp.bfloat16)
    density = jnp.where(keep_own, density_in[None], zero_half)
    perturbed = jnp.where(keep_own, field_terms, zero_half)
    stacked = jnp.concatenate([density, perturbed], 0)
    whole_rows = lax.all_gather(stacked, "orb", axis=2, tiled=True)
    deep_rows = padded_2(whole_rows[0:1], (("aux", 1),), 2 * half_band)
    field_rows = rim_fields(whole_rows[1:], half_band)
    pattern_wide = padded_2(band_pattern, (("aux", 0),), half_band)
    keep_wide = band_keep(pattern_wide, first_row - half_band, total_rows)[None, :, :, None, None]
    density_rims = deep_rows[:, half_band : half_band + count_rows + 2 * half_band]
    cross_term = own_slot_product(whole_rows[0:1], field_rows, my_slot)
    right_term = own_slot_product(whole_rows[1:], density_rims, my_slot)
    first_order = jnp.where(keep_out, cross_term + right_term, 0.0).astype(jnp.bfloat16)
    square_wide = all_slot_product(density_rims, deep_rows)
    square_rims = jnp.where(keep_wide, square_wide, 0.0).astype(jnp.bfloat16)
    square_rows = square_rims[:, half_band : half_band + count_rows]
    order_rows = lax.all_gather(first_order[:, :, None], "orb", axis=2, tiled=True)
    order_rims = rim_fields(order_rows, half_band)
    second = own_slot_product(square_rows, order_rims, my_slot) + own_slot_product(
        order_rows, square_rims, my_slot
    )
    response = jnp.where(keep_out, 2.0 * first_order.astype(jnp.float32) - second, 0.0).astype(
        jnp.bfloat16
    )[:, :, None]
    owner_row = fit_blocks // count_rows
    local_row = fit_blocks % count_rows
    own_piece = jnp.take(response, local_row, axis=1)
    owner_flag = (owner_row == lax.axis_index("aux"))[None, :, None, None, None]
    contrib = jnp.where(owner_flag, own_piece, zero_half).astype(jnp.float32)
    fitted = (
        over_copies(contrib.astype(jnp.bfloat16), "aux").astype(jnp.float32).astype(jnp.bfloat16)
    )
    flat_blocks = fitted.reshape(fitted.shape[0], fitted.shape[1], -1)
    integrals = tensor.reshape(tensor.shape[0], tensor.shape[1], -1)
    partial_value = jnp.einsum(
        "kfm,fpm->fkp", flat_blocks, integrals, preferred_element_type=jnp.float32
    )
    summed = over_copies_2(partial_value, "orb")
    full_sums = gathered_copies(summed, "aux", 2)
    coefficients = jnp.einsum(
        "fpq,fkq->fkp", metric_inv, full_sums, precision=lax.Precision.HIGHEST
    )
    return (response, coefficients)


def solution(mesh):
    in_specs = (
        P("aux", None),
        P("aux", "orb", None, None),
        P(None, "aux", "orb", None, None),
        P(),
        P(None, "aux", "orb", None),
        P(None, "aux", None),
    )
    out_specs = (P(None, "aux", "orb", None, None), P(None, None, "aux"))
    return jax.shard_map(
        on_device, mesh=mesh, in_specs=in_specs, out_specs=out_specs, check_vma=False
    )
```

profile of v0, /device:TPU:1, one launch (start us, length us, event | category | flops | bytes accessed | tf_op | source)
XLA Modules:
  0.0 341.7 jit_solution(3902713181150019706)
XLA Ops:
  11.6 78.4 %all-gather.4.cloned.1.call-done = bf16[3,8,8,128,128]{4,3,1,0,2:T(8,128)(2,1)} async-done(((bf16[3,8,1,128,128]{4,3,1,0,2:T(8,128)(2,1)}), bf16[3,8,8,128,128]{4,3,1,0,2:T(8,128)(2,1)}) %all-gather.4.cloned.1.call-update) | async-done | bytes 6291472 | tf_op jit(solution)/shard_map/all_gather | solution.py:119
  90.0 3.2 slice_bitcast_fusion
  93.2 3.6 %collective-permute-start.2 = (bf16[1,8,8,128,128]{4,3,0,1,2:T(8,128)(2,1)}, bf16[1,8,8,128,128]{4,3,0,1,2:T(8,128)(2,1)}, u32[]{:S(2)}, u32[]{:S(2)}) collective-permute-start(bf16[1,8,8,128,128]{4,3,0,1,2:T(8,128)(2,1)} %slice_bitcast_fusion), channel_id=1, source_target_pairs={{0,8},{8,16},{16,24},{24,32},{32,40},{40,48},{48,56},{56,64},{64,7... | collective-permute-start | bytes 6291464 | tf_op jit(solution)/shard_map/ppermute | solution.py:12
  98.9 2.9 fusion.315
  103.4 3.6 %collective-permute-start = (bf16[2,4,8,128,128]{4,3,0,1,2:T(8,128)(2,1)}, bf16[2,4,8,128,128]{4,3,0,1,2:T(8,128)(2,1)}, u32[]{:S(2)}, u32[]{:S(2)}) collective-permute-start(bf16[2,4,8,128,128]{4,3,0,1,2:T(8,128)(2,1)} %copy.226), channel_id=1, source_target_pairs={{0,8},{8,16},{16,24},{24,32},{32,40},{40,48},{48,56},{56,64},{64,7... | collective-permute-start | bytes 6291464 | tf_op jit(solution)/shard_map/ppermute | solution.py:12
  107.1 2.1 collective-permute-start.1
  111.2 8.9 %collective-permute-done.2 = bf16[1,8,8,128,128]{4,3,0,1,2:T(8,128)(2,1)} collective-permute-done((bf16[1,8,8,128,128]{4,3,0,1,2:T(8,128)(2,1)}, bf16[1,8,8,128,128]{4,3,0,1,2:T(8,128)(2,1)}, u32[]{:S(2)}, u32[]{:S(2)}) %collective-permute-start.2) | collective-permute-done | bytes 2097184 | tf_op jit(solution)/shard_map/ppermute | solution.py:12
  120.1 4.4 %collective-permute-done.3 = bf16[1,8,8,128,128]{4,3,0,1,2:T(8,128)(2,1)} collective-permute-done((bf16[1,8,8,128,128]{4,3,0,1,2:T(8,128)(2,1)}, bf16[1,8,8,128,128]{4,3,0,1,2:T(8,128)(2,1)}, u32[]{:S(2)}, u32[]{:S(2)}) %collective-permute-start.3) | collective-permute-done | bytes 2097184 | tf_op jit(solution)/shard_map/ppermute | solution.py:15
  124.5 3.7 %pad_maximum_fusion = bf16[1,24,8,128,128]{4,3,0,1,2:T(8,128)(2,1)S(1)} fusion(bf16[1,8,8,128,128]{4,3,0,1,2:T(8,128)(2,1)} %collective-permute-done.3, bf16[1,8,8,128,128]{4,3,0,1,2:T(8,128)(2,1)} %slice_bitcast_fusion, bf16[1,8,8,128,128]{4,3,0,1,2:T(8,128)(2,1)} %collective-permute-done.2), kind=kLoop, calls=%fused_computation.4 | loop fusion | flops 6291456 | bytes 12582912 | tf_op jit(solution)/shard_map/concatenate | solution.py:16
  128.2 11.0 %fusion.313 = (bf16[1,16,8,128,128]{4,3,0,1,2:T(8,128)(2,1)}, bf16[16,8,128,128]{3,2,0,1:T(8,128)(2,1)}, bf16[1,16,8,128,128]{4,3,0,1,2:T(8,128)(2,1)}, bf16[1,1...) fusion(bf16[1,24,8,128,128]{4,3,0,1,2:T(8,128)(2,1)S(1)} %pad_m, ...), kind=kLoop, calls=%fused_computation.404 | loop fusion | bytes 62914560 | tf_op jit(solution)/shard_map/slice | solution.py:93
  152.7 4.0 %collective-permute-start.4 = (s32[4,8]{1,0:T(4,128)S(1)}, s32[4,8]{1,0:T(4,128)S(1)}, u32[]{:S(2)}, u32[]{:S(2)}) collective-permute-start(s32[4,8]{1,0:T(4,128)S(1)} %get-tuple-element.43), channel_id=1, source_target_pairs={{0,8},{8,16},{16,24},{24,32},{32,40},{40,48},{48,56},{56,64},{64,7... | collective-permute-start | bytes 392 | tf_op jit(solution)/shard_map/ppermute | solution.py:12
  156.7 2.1 collective-permute-start.5
  161.7 3.7 %fusion.4 = (bf16[16,8,128,128]{3,2,0,1:T(8,128)(2,1)S(1)}, bf16[16,8,128,128]{3,2,0,1:T(8,128)(2,1)S(1)}) fusion(bf16[1,16,8,128,128]{4,3,0,1,2:T(8,128)(2,1)} %get-tuple-element.28, bf16[1,16,8,128,128]{4,3,0,1,2:T(8,128)(2,1)} %get-tuple-element.25), kind=kLoop, calls=%fused_computation.13 | loop fusion | bytes 16777216 | tf_op jit(solution)/shard_map/squeeze | solution.py:94
  165.9 3.4 fusion.2
  170.3 4.3 %fusion.22 = f32[16,128,8,128]{3,1,2,0:T(8,128)} fusion(bf16[1,24,8,128,128]{4,3,0,1,2:T(8,128)(2,1)S(1)} %bitcast.473, bf16[1,16,8,128,128]{4,3,0,1,2:T(8,128)(2,1)S(1)} %copy-done.6), kind=kOutput, calls=%fused_computation.32 | convolution fusion | flops 536870912 | bytes 13107200 | tf_op jit(solution)/shard_map/dot_general | solution.py:94
  174.6 4.5 %fusion.12 = f32[16,128,8,128]{3,1,2,0:T(8,128)} fusion(bf16[16,8,128,128]{3,2,0,1:T(8,128)(2,1)S(1)} %get-tuple-element.48, bf16[1,24,8,128,128]{4,3,0,1,2:T(8,128)(2,1)S(1)} %bitcast.473), kind=kOutput, calls=%fused_computation.22 | convolution fusion | flops 536870912 | bytes 13107200 | tf_op jit(solution)/shard_map/dot_general | solution.py:94
  179.2 4.5 %fusion.14 = f32[16,128,8,128]{3,1,2,0:T(8,128)} fusion(bf16[16,8,128,128]{3,2,0,1:T(8,128)(2,1)S(1)} %get-tuple-element.46, bf16[1,24,8,128,128]{4,3,0,1,2:T(8,128)(2,1)S(1)} %bitcast.473), kind=kOutput, calls=%fused_computation.24 | convolution fusion | flops 536870912 | bytes 13107200 | tf_op jit(solution)/shard_map/dot_general | solution.py:94
  183.6 4.5 %fusion.18 = f32[16,128,8,128]{3,1,2,0:T(8,128)} fusion(bf16[16,8,128,128]{3,2,0,1:T(8,128)(2,1)S(1)} %get-tuple-element.45, bf16[1,24,8,128,128]{4,3,0,1,2:T(8,128)(2,1)S(1)} %bitcast.473), kind=kOutput, calls=%fused_computation.28 | convolution fusion | flops 536870912 | bytes 13107200 | tf_op jit(solution)/shard_map/dot_general | solution.py:94
  188.2 4.5 %fusion.20 = f32[16,128,8,128]{3,1,2,0:T(8,128)} fusion(bf16[16,8,128,128]{3,2,0,1:T(8,128)(2,1)S(1)} %get-tuple-element.47, bf16[1,24,8,128,128]{4,3,0,1,2:T(8,128)(2,1)S(1)} %bitcast.473), kind=kOutput, calls=%fused_computation.30 | convolution fusion | flops 536870912 | bytes 13107200 | tf_op jit(solution)/shard_map/dot_general | solution.py:94
  192.7 4.5 %fusion.16 = f32[16,128,8,128]{3,1,2,0:T(8,128)} fusion(bf16[16,8,128,128]{3,2,0,1:T(8,128)(2,1)S(1)} %copy-done.5, bf16[1,24,8,128,128]{4,3,0,1,2:T(8,128)(2,1)S(1)} %bitcast.473), kind=kOutput, calls=%fused_computation.26 | convolution fusion | flops 536870912 | bytes 13107200 | tf_op jit(solution)/shard_map/dot_general | solution.py:94
  197.2 5.9 %fusion.24 = f32[16,128,8,128]{3,1,2,0:T(8,128)} fusion(bf16[1,24,8,128,128]{4,3,0,1,2:T(8,128)(2,1)S(1)} %bitcast.473, bf16[1,8,8,128,128]{4,3,0,1,2:T(8,128)(2,1)} %slice_bitcast_fusion, bf16[1,8,8,128,128]{4,3,0,1,2:T(8,128)(2,1)} %collective-permute-done.2), kind=kOutput, calls=%fused_computation.34 | convolution fusion | flops 553648128 | bytes 13107200 | tf_op jit(solution)/shard_map/dot_general | solution.py:94
  203.1 4.2 %all-gather.6.cloned.1.call-done = bf16[2,8,1024,128]{3,2,0,1:T(8,128)(2,1)} async-done(((bf16[2,8,128,128]{3,2,0,1:T(8,128)(2,1)}), bf16[2,8,1024,128]{3,2,0,1:T(8,128)(2,1)}) %all-gather.6.cloned.1.call-update) | async-done | bytes 4194320 | tf_op jit(solution)/shard_map/all_gather | solution.py:131
  207.2 5.1 %fusion.316 = (bf16[2,4,8,128,128]{4,3,0,1,2:T(8,128)(2,1)}, bf16[2,4,8,128,128]{4,3,0,1,2:T(8,128)(2,1)}) fusion(bf16[2,8,8,128,128]{4,3,2,0,1:T(8,128)(2,1)} %bitcast.476), kind=kLoop, calls=%fused_computation.407 | loop fusion | bytes 8388608 | tf_op jit(solution)/shard_map/slice | solution.py:15
  212.3 3.8 %collective-permute-start.6 = (bf16[2,4,8,128,128]{4,3,0,1,2:T(8,128)(2,1)}, bf16[2,4,8,128,128]{4,3,0,1,2:T(8,128)(2,1)S(1)}, u32[]{:S(2)}, u32[]{:S(2)}) collective-permute-start(bf16[2,4,8,128,128]{4,3,0,1,2:T(8,128)(2,1)} %get-tuple-element.42), channel_id=1, source_target_pairs={{0,8},{8,16},{16,24},{24,32},{32,40},{40,48},{48,56},{56,64},{64,7... | collective-permute-start | bytes 6291464 | tf_op jit(solution)/shard_map/ppermute | solution.py:12
  216.1 20.1 %select_convert_fusion = bf16[16,128,8,128]{3,1,2,0:T(8,128)(2,1)} fusion(f32[16,128,8,128]{3,1,2,0:T(8,128)} %fusion.12, f32[16,128,8,128]{3,1,2,0:T(8,128)} %fusion.14, f32[16,128,8,128]{3,1,2,0:T(8,128)} %fusion.16, f32[16,128,8,128]{3,1,2,0:T(8,128)} %fusion.18, f32[16,128,8,128]{3,1,2,0:T(8,128)S(1)} %copy-done.3, f32[16,128,8,128]{3,1,2,0:T(8,128)} %fusion.24, ...), kind=kOutput, calls=%fused_computation.3 | convolution fusion | flops 555745280 | bytes 67633280 | tf_op jit(solution)/shard_map/dot_general | solution.py:94
  236.2 2.4 collective-permute-start.7
  243.5 20.5 %collective-permute-done.7 = bf16[2,4,8,128,128]{4,3,0,1,2:T(8,128)(2,1)S(1)} collective-permute-done((bf16[2,4,8,128,128]{4,3,0,1,2:T(8,128)(2,1)}, bf16[2,4,8,128,128]{4,3,0,1,2:T(8,128)(2,1)S(1)}, u32[]{:S(2)}, u32[]{:S(2)}) %collective-permute-start.7) | collective-permute-done | bytes 2097184 | tf_op jit(solution)/shard_map/ppermute | solution.py:15
  268.6 36.8 %all_to_all.15 = bf16[32,2,1,1,128,128]{5,4,3,2,1,0:T(8,128)(2,1)} all-to-all(bf16[32,2,1,1,128,128]{5,4,3,2,1,0:T(8,128)(2,1)S(1)} %broadcast_in_dim.168), channel_id=1, replica_groups=mesh['aux'=32,'orb'=8] {'aux'}, dimensions={0} | all-to-all | bytes 4194304 | tf_op jit(solution)/shard_map/all_to_all | solution.py:22
  308.2 10.4 %all_to_all.16 = f32[8,1,2,96]{3,2,1,0:T(2,128)S(1)} all-to-all(f32[8,1,2,96]{3,2,1,0:T(2,128)S(1)} %broadcast_in_dim.169), channel_id=1, replica_groups=mesh['aux'=32,'orb'=8] {'orb'}, dimensions={0} | all-to-all | bytes 12288 | tf_op jit(solution)/shard_map/all_to_all | solution.py:22
  319.3 5.3 %all-to-all-start.2 = ((f32[32,1,2,96]{3,2,1,0:T(2,128)}), f32[32,1,2,96]{3,2,1,0:T(2,128)S(1)}, u32[]{:S(2)}, u32[]{:S(2)}) async-start(f32[32,1,2,96]{3,2,1,0:T(2,128)} %broadcast_in_dim.170), calls=%async_computation.2 | async-start | bytes 65536 | tf_op jit(solution)/shard_map/all_to_all | solution.py:22
  326.5 5.5 %all-to-all-done.2 = f32[32,1,2,96]{3,2,1,0:T(2,128)S(1)} async-done(((f32[32,1,2,96]{3,2,1,0:T(2,128)}), f32[32,1,2,96]{3,2,1,0:T(2,128)S(1)}, u32[]{:S(2)}, u32[]{:S(2)}) %all-to-all-start.2) | async-done | bytes 24608 | tf_op jit(solution)/shard_map/all_to_all | solution.py:22
  332.0 2.9 fusion.43
  (115 shorter events, 41.7 us)
Async XLA Ops:
  7.2 300.2 %copy-start = (bf16[1,96,1,16384]{3,1,2,0:T(8,128)(2,1)S(1)}, bf16[1,96,1,16384]{3,1,2,0:T(8,128)(2,1)}, u32[]{:S(2)}) copy-start(bf16[1,96,1,16384]{3,1,2,0:T(8,128)(2,1)} %param.10) | copy-start | bytes 9437188
  7.2 82.8 %all-gather.4.cloned.1.call-start = ((), (), s32[]{:S(2)}) async-start(), calls=%async_computation.3 | async-start | bytes 7077888 | tf_op jit(solution)/shard_map/all_gather | solution.py:119
  11.6 195.7 %all-gather.6.cloned.1.call-start = ((), (), s32[]{:S(2)}) async-start(), calls=%async_computation.4 | async-start | bytes 4718592 | tf_op jit(solution)/shard_map/all_gather | solution.py:131
  93.2 26.9 %collective-permute-start.2 = (bf16[1,8,8,128,128]{4,3,0,1,2:T(8,128)(2,1)}, bf16[1,8,8,128,128]{4,3,0,1,2:T(8,128)(2,1)}, u32[]{:S(2)}, u32[]{:S(2)}) collective-permute-start(bf16[1,8,8,128,128]{4,3,0,1,2:T(8,128)(2,1)} %slice_bitcast_fusion), channel_id=1, source_target_pairs={{0,8},{8,16},{16,24},{24,32},{32,40},{40,48},{48,56},{56,64},{64,7... | collective-permute-start | bytes 6291464 | tf_op jit(solution)/shard_map/ppermute | solution.py:12
  96.9 27.7 %collective-permute-start.3 = (bf16[1,8,8,128,128]{4,3,0,1,2:T(8,128)(2,1)}, bf16[1,8,8,128,128]{4,3,0,1,2:T(8,128)(2,1)}, u32[]{:S(2)}, u32[]{:S(2)}) collective-permute-start(bf16[1,8,8,128,128]{4,3,0,1,2:T(8,128)(2,1)} %slice_bitcast_fusion), channel_id=1, source_target_pairs={{8,0},{16,8},{24,16},{32,24},{40,32},{48,40},{56,48},{64,56},{72,6... | collective-permute-start | bytes 6291464 | tf_op jit(solution)/shard_map/ppermute | solution.py:15
  98.9 10.4 %slice-start.2 = ((s8[6291456]{0:T(1024)(128)(4,1)}), s8[4194304]{0:T(1024)(128)(4,1)S(1)}, s32[]{:S(2)}) async-start(s8[6291456]{0:T(1024)(128)(4,1)} %bitcast.474), calls=%async_computation.7 | async-start | bytes 8388608
  101.8 7.5 %slice-start.3 = ((s8[6291456]{0:T(1024)(128)(4,1)}), s8[2097152]{0:T(1024)(128)(4,1)S(1)}, s32[]{:S(2)}) async-start(s8[6291456]{0:T(1024)(128)(4,1)} %bitcast.474), calls=%async_computation.8 | async-start | bytes 4194304
  103.4 39.2 %collective-permute-start = (bf16[2,4,8,128,128]{4,3,0,1,2:T(8,128)(2,1)}, bf16[2,4,8,128,128]{4,3,0,1,2:T(8,128)(2,1)}, u32[]{:S(2)}, u32[]{:S(2)}) collective-permute-start(bf16[2,4,8,128,128]{4,3,0,1,2:T(8,128)(2,1)} %copy.226), channel_id=1, source_target_pairs={{0,8},{8,16},{16,24},{24,32},{32,40},{40,48},{48,56},{56,64},{64,7... | collective-permute-start | bytes 6291464 | tf_op jit(solution)/shard_map/ppermute | solution.py:12
  107.1 39.9 %collective-permute-start.1 = (bf16[2,4,8,128,128]{4,3,0,1,2:T(8,128)(2,1)S(1)}, bf16[2,4,8,128,128]{4,3,0,1,2:T(8,128)(2,1)}, u32[]{:S(2)}, u32[]{:S(2)}) collective-permute-start(bf16[2,4,8,128,128]{4,3,0,1,2:T(8,128)(2,1)S(1)} %copy.228), channel_id=1, source_target_pairs={{8,0},{16,8},{24,16},{32,24},{40,32},{48,40},{56,48},{64,56},{72,6... | collective-permute-start | bytes 6291464 | tf_op jit(solution)/shard_map/ppermute | solution.py:15
  128.2 11.5 %copy-start.1 = (bf16[1,24,8,128,128]{4,3,0,1,2:T(8,128)(2,1)}, bf16[1,24,8,128,128]{4,3,0,1,2:T(8,128)(2,1)S(1)}, u32[]{:S(2)}) copy-start(bf16[1,24,8,128,128]{4,3,0,1,2:T(8,128)(2,1)S(1)} %pad_maximum_fusion) | copy-start | bytes 18874372
  139.6 4.7 %copy-start.15 = (bf16[2,8,1,128,128]{4,3,1,0,2:T(8,128)(2,1)S(1)}, bf16[2,8,1,128,128]{4,3,1,0,2:T(8,128)(2,1)}, u32[]{:S(2)}) copy-start(bf16[2,8,1,128,128]{4,3,1,0,2:T(8,128)(2,1)} %get-tuple-element.35) | copy-start | bytes 1572868
  141.3 3.4 copy-start.14
  141.3 3.7 %copy-start.13 = (bf16[2,8,1,128,128]{4,3,1,0,2:T(8,128)(2,1)S(1)}, bf16[2,8,1,128,128]{4,3,1,0,2:T(8,128)(2,1)}, u32[]{:S(2)}) copy-start(bf16[2,8,1,128,128]{4,3,1,0,2:T(8,128)(2,1)} %get-tuple-element.33) | copy-start | bytes 1572868
  144.3 1.0 copy-start.12
  144.7 1.1 copy-start.11
  150.5 1.0 copy-start.10
  150.8 1.9 copy-start.16
  152.7 6.8 %collective-permute-start.4 = (s32[4,8]{1,0:T(4,128)S(1)}, s32[4,8]{1,0:T(4,128)S(1)}, u32[]{:S(2)}, u32[]{:S(2)}) collective-permute-start(s32[4,8]{1,0:T(4,128)S(1)} %get-tuple-element.43), channel_id=1, source_target_pairs={{0,8},{8,16},{16,24},{24,32},{32,40},{40,48},{48,56},{56,64},{64,7... | collective-permute-start | bytes 392 | tf_op jit(solution)/shard_map/ppermute | solution.py:12
  156.7 4.9 %collective-permute-start.5 = (s32[4,8]{1,0:T(4,128)S(1)}, s32[4,8]{1,0:T(4,128)S(1)}, u32[]{:S(2)}, u32[]{:S(2)}) collective-permute-start(s32[4,8]{1,0:T(4,128)S(1)} %get-tuple-element.44), channel_id=1, source_target_pairs={{8,0},{16,8},{24,16},{32,24},{40,32},{48,40},{56,48},{64,56},{72,6... | collective-permute-start | bytes 392 | tf_op jit(solution)/shard_map/ppermute | solution.py:15
  161.7 4.2 %copy-start.7 = (bf16[1,16,8,128,128]{4,3,0,1,2:T(8,128)(2,1)S(1)}, bf16[1,16,8,128,128]{4,3,0,1,2:T(8,128)(2,1)}, u32[]{:S(2)}) copy-start(bf16[1,16,8,128,128]{4,3,0,1,2:T(8,128)(2,1)} %get-tuple-element.26) | copy-start | bytes 12582916
  161.7 7.6 %slice-start = ((s8[6291456]{0:T(1024)(128)(4,1)}), s8[4194304]{0:T(1024)(128)(4,1)S(1)}, s32[]{:S(2)}) async-start(s8[6291456]{0:T(1024)(128)(4,1)} %bitcast.472), calls=%async_computation.5 | async-start | bytes 8388608
  165.4 4.9 %slice-start.1 = ((s8[6291456]{0:T(1024)(128)(4,1)}), s8[2097152]{0:T(1024)(128)(4,1)S(1)}, s32[]{:S(2)}) async-start(s8[6291456]{0:T(1024)(128)(4,1)} %bitcast.472), calls=%async_computation.6 | async-start | bytes 4194304
  165.9 4.4 %copy-start.6 = (bf16[1,16,8,128,128]{4,3,0,1,2:T(8,128)(2,1)S(1)}, bf16[1,16,8,128,128]{4,3,0,1,2:T(8,128)(2,1)}, u32[]{:S(2)}) copy-start(bf16[1,16,8,128,128]{4,3,0,1,2:T(8,128)(2,1)} %get-tuple-element.29) | copy-start | bytes 12582916
  188.2 4.5 %copy-start.5 = (bf16[16,8,128,128]{3,2,0,1:T(8,128)(2,1)S(1)}, bf16[16,8,128,128]{3,2,0,1:T(8,128)(2,1)}, u32[]{:S(2)}) copy-start(bf16[16,8,128,128]{3,2,0,1:T(8,128)(2,1)} %get-tuple-element.24) | copy-start | bytes 12582916
  207.2 8.9 %copy-start.3 = (f32[16,128,8,128]{3,1,2,0:T(8,128)S(1)}, f32[16,128,8,128]{3,1,2,0:T(8,128)}, u32[]{:S(2)}) copy-start(f32[16,128,8,128]{3,1,2,0:T(8,128)} %fusion.20) | copy-start | bytes 25165828
  212.3 30.3 %collective-permute-start.6 = (bf16[2,4,8,128,128]{4,3,0,1,2:T(8,128)(2,1)}, bf16[2,4,8,128,128]{4,3,0,1,2:T(8,128)(2,1)S(1)}, u32[]{:S(2)}, u32[]{:S(2)}) collective-permute-start(bf16[2,4,8,128,128]{4,3,0,1,2:T(8,128)(2,1)} %get-tuple-element.42), channel_id=1, source_target_pairs={{0,8},{8,16},{16,24},{24,32},{32,40},{40,48},{48,56},{56,64},{64,7... | collective-permute-start | bytes 6291464 | tf_op jit(solution)/shard_map/ppermute | solution.py:12
  216.1 22.5 %copy-start.2 = (bf16[2,8,1024,128]{3,2,0,1:T(8,128)(2,1)S(1)}, bf16[2,8,1024,128]{3,2,0,1:T(8,128)(2,1)}, u32[]{:S(2)}) copy-start(bf16[2,8,1024,128]{3,2,0,1:T(8,128)(2,1)} %all-gather.6.cloned.1.call-done) | copy-start | bytes 12582916
  236.2 4.9 %copy-start.4 = (bf16[16,128,8,128]{3,1,2,0:T(8,128)(2,1)S(1)}, bf16[16,128,8,128]{3,1,2,0:T(8,128)(2,1)}, u32[]{:S(2)}) copy-start(bf16[16,128,8,128]{3,1,2,0:T(8,128)(2,1)} %select_convert_fusion) | copy-start | bytes 12582916
  236.2 27.8 %collective-permute-start.7 = (bf16[2,4,8,128,128]{4,3,0,1,2:T(8,128)(2,1)}, bf16[2,4,8,128,128]{4,3,0,1,2:T(8,128)(2,1)S(1)}, u32[]{:S(2)}, u32[]{:S(2)}) collective-permute-start(bf16[2,4,8,128,128]{4,3,0,1,2:T(8,128)(2,1)} %get-tuple-element.41), channel_id=1, source_target_pairs={{8,0},{16,8},{24,16},{32,24},{40,32},{48,40},{56,48},{64,56},{72,6... | collective-permute-start | bytes 6291464 | tf_op jit(solution)/shard_map/ppermute | solution.py:15
  265.8 1.0 copy-start.8
  267.3 0.8 copy-start.9
  319.3 12.6 %all-to-all-start.2 = ((f32[32,1,2,96]{3,2,1,0:T(2,128)}), f32[32,1,2,96]{3,2,1,0:T(2,128)S(1)}, u32[]{:S(2)}, u32[]{:S(2)}) async-start(f32[32,1,2,96]{3,2,1,0:T(2,128)} %broadcast_in_dim.170), calls=%async_computation.2 | async-start | bytes 65536 | tf_op jit(solution)/shard_map/all_to_all | solution.py:22
Sparse Core Ops, SparseCore 0:
  11.7 78.2 all-gather.3
  152.8 54.4 all-gather.5
where the time goes:
time: 343 us; the launch traced here: 342 us
  waiting for transfers between devices  126 us (37%)
  matrix products  69.8 us (20%)
  blocking collectives  47.2 us (14%)
  local copies, waits for them, and re-layouts  45.7 us (13%)
  starting transfers between devices  29 us (8%)
  between operations  15.5 us (5%)
  other arithmetic  8.87 us (3%)
    all_gather x1, waiting for transfers between devices, on_device(): whole_rows = lax.all_gather(stacked, 'orb', axis=2, tiled=True)  78.4 us
    dot_general x8, matrix products, all_slot_product(): jnp.matmul(factor_left[:, :, stride:stride + 1], source, preferred_elemen...  52.8 us
    all_to_all x2, blocking collectives, sent_to_all(): return lax.all_to_all(copies, axis, split_axis=0, concat_axis=0, tiled=True)  47.2 us
    ppermute x4, waiting for transfers between devices, padded_2(): lax.ppermute(lax.slice_in_dim(block, 0, width, axis=dim), axis, backward)  27.4 us
    ppermute x4, starting transfers between devices, padded_2(): lax.ppermute(lax.slice_in_dim(block, block.shape[dim] - width, None, axis...  15 us
    dot_general x32, matrix products, own_slot_product(): jnp.matmul(factor_left[:, :, stride], picked, preferred_element_type=jnp....  13.2 us
    unnamed x50, local copies, waits for them, and re-layouts  13.2 us
    slice x1, local copies, waits for them, and re-layouts, all_slot_product(): right_rims[:, stride:stride + count_rows]  11 us
  transfers between devices with their start and end apart: 11, of which 9 were waited for; matrix products, arithmetic and copies ran while one was open for 27% of the time, Pallas kernels for 0%

commit v1 on v0

--- a/solution.py
+++ b/solution.py
@@ -116,7 +116,9 @@
     density = jnp.where(keep_own, density_in[None], zero_half)
     perturbed = jnp.where(keep_own, field_terms, zero_half)
     stacked = jnp.concatenate([density, perturbed], 0)
-    whole_rows = lax.all_gather(stacked, "orb", axis=2, tiled=True)
+    whole_rows = jnp.concatenate(
+        lax.all_to_all(jnp.stack([stacked] * lax.axis_size("orb")), "orb", 0, 0), axis=2
+    )
     deep_rows = padded_2(whole_rows[0:1], (("aux", 1),), 2 * half_band)
     field_rows = rim_fields(whole_rows[1:], half_band)
     pattern_wide = padded_2(band_pattern, (("aux", 0),), half_band)

time: 343 us -> 422 us (1.23)
  blocking collectives: 47.2 us -> 196 us
  waiting for transfers between devices: 126 us -> 53.4 us
  local copies, waits for them, and re-layouts: 45.7 us -> 38.7 us
  matrix products: 69.8 us -> 76.4 us
    all_to_all x0 -> x1, blocking collectives: none -> 148 us  [on_device(): lax.all_to_all(jnp.stack([stacked] * lax.axis_size('orb')), 'orb', 0, 0)]
    all_gather x1 -> x0, waiting for transfers between devices: 78.4 us -> none  [on_device(): whole_rows = lax.all_gather(stacked, 'orb', axis=2, tiled=True)]
    dot_general x32, matrix products: 13.2 us -> 19.8 us  [own_slot_product(): jnp.matmul(factor_left[:, :, stride], picked, preferred_element_type=jnp....]
    unnamed x50 -> x33, local copies, waits for them, and re-layouts: 13.2 us -> 8.05 us
  transfers between devices with their start and end apart: 11 -> 10, of which waited for: 9 -> 8; matrix products, arithmetic and copies ran while one was open for 27% -> 20% of each run, Pallas kernels for 0% -> 0%
where the time goes in v1:
time: 422 us; the launch traced here: 421 us
  blocking collectives  196 us (46%)
  matrix products  76.4 us (18%)
  waiting for transfers between devices  53.4 us (13%)
  local copies, waits for them, and re-layouts  38.7 us (9%)
  starting transfers between devices  29.1 us (7%)
  between operations  15.4 us (4%)
  other arithmetic  12.2 us (3%)
    all_to_all x1, blocking collectives, on_device(): lax.all_to_all(jnp.stack([stacked] * lax.axis_size('orb')), 'orb', 0, 0)  148 us
    dot_general x8, matrix products, all_slot_product(): jnp.matmul(factor_left[:, :, stride:stride + 1], source, preferred_elemen...  52.8 us
    all_to_all x2, blocking collectives, sent_to_all(): return lax.all_to_all(copies, axis, split_axis=0, concat_axis=0, tiled=True)  47.2 us
    ppermute x4, waiting for transfers between devices, padded_2(): lax.ppermute(lax.slice_in_dim(block, 0, width, axis=dim), axis, backward)  30.9 us
    dot_general x32, matrix products, own_slot_product(): jnp.matmul(factor_left[:, :, stride], picked, preferred_element_type=jnp....  19.8 us
    ppermute x4, starting transfers between devices, padded_2(): lax.ppermute(lax.slice_in_dim(block, block.shape[dim] - width, None, axis...  14.8 us
    ppermute x4, waiting for transfers between devices, padded_2(): lax.ppermute(lax.slice_in_dim(block, block.shape[dim] - width, None, axis...  12.9 us
    slice x1, local copies, waits for them, and re-layouts, all_slot_product(): right_rims[:, stride:stride + count_rows]  10.6 us
  transfers between devices with their start and end apart: 10, of which 8 were waited for; matrix products, arithmetic and copies ran while one was open for 20% of the time, Pallas kernels for 0%

profile of v1, /device:TPU:1, one launch (start us, length us, event | category | flops | bytes accessed | tf_op | source)
XLA Modules:
  0.0 420.7 jit_solution(14130313957078165435)
XLA Ops:
  12.3 148.4 %all_to_all.20 = bf16[8,3,8,1,128,128]{5,4,1,2,3,0:T(8,128)(2,1)S(1)} all-to-all(bf16[8,3,8,1,128,128]{5,4,1,2,3,0:T(8,128)(2,1)S(1)} %stack.2), channel_id=1, replica_groups=mesh['aux'=32,'orb'=8] {'orb'}, dimensions={0} | all-to-all | bytes 12582912 | tf_op jit(solution)/shard_map/all_to_all | solution.py:120
  162.2 5.4 %collective-permute-start.2 = (bf16[1,8,8,128,128]{4,3,1,2,0:T(8,128)(2,1)}, bf16[1,8,8,128,128]{4,3,1,2,0:T(8,128)(2,1)}, u32[]{:S(2)}, u32[]{:S(2)}) collective-permute-start(bf16[1,8,8,128,128]{4,3,1,2,0:T(8,128)(2,1)} %slice_bitcast_fusion.1), channel_id=1, source_target_pairs={{0,8},{8,16},{16,24},{24,32},{32,40},{40,48},{48,56},{56,64},{64,7... | collective-permute-start | bytes 6291464 | tf_op jit(solution)/shard_map/ppermute | solution.py:12
  170.1 2.4 fusion.316
  173.6 3.6 collective-permute-start
  177.3 2.1 collective-permute-start.1
  179.4 11.5 %collective-permute-done.2 = bf16[1,8,8,128,128]{4,3,1,2,0:T(8,128)(2,1)} collective-permute-done((bf16[1,8,8,128,128]{4,3,1,2,0:T(8,128)(2,1)}, bf16[1,8,8,128,128]{4,3,1,2,0:T(8,128)(2,1)}, u32[]{:S(2)}, u32[]{:S(2)}) %collective-permute-start.2) | collective-permute-done | bytes 2097184 | tf_op jit(solution)/shard_map/ppermute | solution.py:12
  190.9 4.4 %collective-permute-done.3 = bf16[1,8,8,128,128]{4,3,1,2,0:T(8,128)(2,1)} collective-permute-done((bf16[1,8,8,128,128]{4,3,1,2,0:T(8,128)(2,1)}, bf16[1,8,8,128,128]{4,3,1,2,0:T(8,128)(2,1)}, u32[]{:S(2)}, u32[]{:S(2)}) %collective-permute-start.3) | collective-permute-done | bytes 2097184 | tf_op jit(solution)/shard_map/ppermute | solution.py:15
  195.3 3.7 pad_maximum_fusion.1
  199.0 10.6 %fusion.314 = (bf16[1,16,8,128,128]{4,3,1,2,0:T(8,128)(2,1)}, bf16[16,8,128,128]{3,2,0,1:T(8,128)(2,1)}, bf16[1,16,8,128,128]{4,3,1,2,0:T(8,128)(2,1)}, bf16[1,1...) fusion(bf16[1,24,8,128,128]{4,3,1,2,0:T(8,128)(2,1)S(1)} %pad_m, ...), kind=kLoop, calls=%fused_computation.404 | loop fusion | bytes 62914560 | tf_op jit(solution)/shard_map/slice | solution.py:93
  213.4 4.4 %collective-permute-done.1 = bf16[2,4,8,128,128]{4,3,0,1,2:T(8,128)(2,1)} collective-permute-done((bf16[2,4,8,128,128]{4,3,0,1,2:T(8,128)(2,1)}, bf16[2,4,8,128,128]{4,3,0,1,2:T(8,128)(2,1)}, u32[]{:S(2)}, u32[]{:S(2)}) %collective-permute-start.1) | collective-permute-done | bytes 2097184 | tf_op jit(solution)/shard_map/ppermute | solution.py:15
  217.8 3.3 pad_maximum_fusion
  235.6 2.6 collective-permute-start.5
  240.6 3.7 fusion.4
  244.9 3.4 fusion.2
  249.3 4.3 %fusion.22 = f32[16,128,8,128]{3,1,2,0:T(8,128)} fusion(bf16[1,24,8,128,128]{4,3,1,2,0:T(8,128)(2,1)S(1)} %bitcast.468, bf16[1,16,8,128,128]{4,3,1,2,0:T(8,128)(2,1)S(1)} %copy-done.8), kind=kOutput, calls=%fused_computation.33 | convolution fusion | flops 536870912 | bytes 13107200 | tf_op jit(solution)/shard_map/dot_general | solution.py:94
  253.6 4.5 %fusion.20 = f32[16,128,8,128]{3,1,2,0:T(8,128)} fusion(bf16[16,8,128,128]{3,2,0,1:T(8,128)(2,1)S(1)} %get-tuple-element.39, bf16[1,24,8,128,128]{4,3,1,2,0:T(8,128)(2,1)S(1)} %bitcast.468), kind=kOutput, calls=%fused_computation.31 | convolution fusion | flops 536870912 | bytes 13107200 | tf_op jit(solution)/shard_map/dot_general | solution.py:94
  258.1 4.5 %fusion.18 = f32[16,128,8,128]{3,1,2,0:T(8,128)} fusion(bf16[16,8,128,128]{3,2,0,1:T(8,128)(2,1)S(1)} %get-tuple-element.37, bf16[1,24,8,128,128]{4,3,1,2,0:T(8,128)(2,1)S(1)} %bitcast.468), kind=kOutput, calls=%fused_computation.29 | convolution fusion | flops 536870912 | bytes 13107200 | tf_op jit(solution)/shard_map/dot_general | solution.py:94
  262.6 4.5 %fusion.14 = f32[16,128,8,128]{3,1,2,0:T(8,128)} fusion(bf16[16,8,128,128]{3,2,0,1:T(8,128)(2,1)S(1)} %get-tuple-element.38, bf16[1,24,8,128,128]{4,3,1,2,0:T(8,128)(2,1)S(1)} %bitcast.468), kind=kOutput, calls=%fused_computation.25 | convolution fusion | flops 536870912 | bytes 13107200 | tf_op jit(solution)/shard_map/dot_general | solution.py:94
  267.1 4.5 %fusion.12 = f32[16,128,8,128]{3,1,2,0:T(8,128)} fusion(bf16[16,8,128,128]{3,2,0,1:T(8,128)(2,1)S(1)} %get-tuple-element.40, bf16[1,24,8,128,128]{4,3,1,2,0:T(8,128)(2,1)S(1)} %bitcast.468), kind=kOutput, calls=%fused_computation.23 | convolution fusion | flops 536870912 | bytes 13107200 | tf_op jit(solution)/shard_map/dot_general | solution.py:94
  271.6 4.5 %fusion.16 = f32[16,128,8,128]{3,1,2,0:T(8,128)} fusion(bf16[16,8,128,128]{3,2,0,1:T(8,128)(2,1)S(1)} %copy-done.7, bf16[1,24,8,128,128]{4,3,1,2,0:T(8,128)(2,1)S(1)} %bitcast.468), kind=kOutput, calls=%fused_computation.27 | convolution fusion | flops 536870912 | bytes 13107200 | tf_op jit(solution)/shard_map/dot_general | solution.py:94
  276.1 5.9 %fusion.24 = f32[16,128,8,128]{3,1,2,0:T(8,128)} fusion(bf16[1,24,8,128,128]{4,3,1,2,0:T(8,128)(2,1)S(1)} %bitcast.468, bf16[1,8,8,128,128]{4,3,1,2,0:T(8,128)(2,1)} %slice_bitcast_fusion.1, bf16[1,8,8,128,128]{4,3,1,2,0:T(8,128)(2,1)} %collective-permute-done.2), kind=kOutput, calls=%fused_computation.35 | convolution fusion | flops 553648128 | bytes 13107200 | tf_op jit(solution)/shard_map/dot_general | solution.py:94
  281.9 4.1 all-gather.3.cloned.1.call-done
  286.1 5.1 %fusion.315 = (bf16[2,4,8,128,128]{4,3,0,1,2:T(8,128)(2,1)}, bf16[2,4,8,128,128]{4,3,0,1,2:T(8,128)(2,1)}) fusion(bf16[2,8,8,128,128]{4,3,2,0,1:T(8,128)(2,1)} %bitcast.469), kind=kLoop, calls=%fused_computation.405 | loop fusion | bytes 8388608 | tf_op jit(solution)/shard_map/slice | solution.py:15
  291.1 3.8 collective-permute-start.6
  294.9 20.2 %select_convert_fusion = bf16[16,128,8,128]{3,1,2,0:T(8,128)(2,1)} fusion(f32[16,128,8,128]{3,1,2,0:T(8,128)S(1)} %copy-done.5, f32[16,128,8,128]{3,1,2,0:T(8,128)} %fusion.14, f32[16,128,8,128]{3,1,2,0:T(8,128)} %fusion.16, f32[16,128,8,128]{3,1,2,0:T(8,128)} %fusion.18, f32[16,128,8,128]{3,1,2,0:T(8,128)} %fusion.20, f32[16,128,8,128]{3,1,2,0:T(8,128)} %fusion.24, ...), kind=kOutput, calls=%fused_computation.4 | convolution fusion | flops 555745280 | bytes 67633280 | tf_op jit(solution)/shard_map/dot_general | solution.py:94
  315.1 2.4 collective-permute-start.7
  322.4 20.5 %collective-permute-done.7 = bf16[2,4,8,128,128]{4,3,0,1,2:T(8,128)(2,1)S(1)} collective-permute-done((bf16[2,4,8,128,128]{4,3,0,1,2:T(8,128)(2,1)}, bf16[2,4,8,128,128]{4,3,0,1,2:T(8,128)(2,1)S(1)}, u32[]{:S(2)}, u32[]{:S(2)}) %collective-permute-start.7) | collective-permute-done | bytes 2097184 | tf_op jit(solution)/shard_map/ppermute | solution.py:15
  347.5 36.8 %all_to_all.21 = bf16[32,2,1,1,128,128]{5,4,3,2,1,0:T(8,128)(2,1)} all-to-all(bf16[32,2,1,1,128,128]{5,4,3,2,1,0:T(8,128)(2,1)S(1)} %broadcast_in_dim.168), channel_id=1, replica_groups=mesh['aux'=32,'orb'=8] {'aux'}, dimensions={0} | all-to-all | bytes 4194304 | tf_op jit(solution)/shard_map/all_to_all | solution.py:22
  387.2 10.4 %all_to_all.22 = f32[8,1,2,96]{3,2,1,0:T(2,128)S(1)} all-to-all(f32[8,1,2,96]{3,2,1,0:T(2,128)S(1)} %broadcast_in_dim.169), channel_id=1, replica_groups=mesh['aux'=32,'orb'=8] {'orb'}, dimensions={0} | all-to-all | bytes 12288 | tf_op jit(solution)/shard_map/all_to_all | solution.py:22
  398.2 5.3 %all-to-all-start.3 = ((f32[32,1,2,96]{3,2,1,0:T(2,128)}), f32[32,1,2,96]{3,2,1,0:T(2,128)S(1)}, u32[]{:S(2)}, u32[]{:S(2)}) async-start(f32[32,1,2,96]{3,2,1,0:T(2,128)} %broadcast_in_dim.170), calls=%async_computation.3 | async-start | bytes 65536 | tf_op jit(solution)/shard_map/all_to_all | solution.py:22
  405.4 5.5 %all-to-all-done.3 = f32[32,1,2,96]{3,2,1,0:T(2,128)S(1)} async-done(((f32[32,1,2,96]{3,2,1,0:T(2,128)}), f32[32,1,2,96]{3,2,1,0:T(2,128)S(1)}, u32[]{:S(2)}, u32[]{:S(2)}) %all-to-all-start.3) | async-done | bytes 24608 | tf_op jit(solution)/shard_map/all_to_all | solution.py:22
  411.0 2.9 fusion.43
  (96 shorter events, 46.2 us)
Async XLA Ops:
  7.2 379.1 %copy-start = (bf16[1,96,1,16384]{3,1,2,0:T(8,128)(2,1)S(1)}, bf16[1,96,1,16384]{3,1,2,0:T(8,128)(2,1)}, u32[]{:S(2)}) copy-start(bf16[1,96,1,16384]{3,1,2,0:T(8,128)(2,1)} %param.10) | copy-start | bytes 9437188
  7.2 278.9 %all-gather.3.cloned.1.call-start = ((), (), s32[]{:S(2)}) async-start(), calls=%async_computation.4 | async-start | bytes 4718592 | tf_op jit(solution)/shard_map/all_gather | solution.py:133
  162.2 28.7 %collective-permute-start.2 = (bf16[1,8,8,128,128]{4,3,1,2,0:T(8,128)(2,1)}, bf16[1,8,8,128,128]{4,3,1,2,0:T(8,128)(2,1)}, u32[]{:S(2)}, u32[]{:S(2)}) collective-permute-start(bf16[1,8,8,128,128]{4,3,1,2,0:T(8,128)(2,1)} %slice_bitcast_fusion.1), channel_id=1, source_target_pairs={{0,8},{8,16},{16,24},{24,32},{32,40},{40,48},{48,56},{56,64},{64,7... | collective-permute-start | bytes 6291464 | tf_op jit(solution)/shard_map/ppermute | solution.py:12
  167.6 27.7 %collective-permute-start.3 = (bf16[1,8,8,128,128]{4,3,1,2,0:T(8,128)(2,1)}, bf16[1,8,8,128,128]{4,3,1,2,0:T(8,128)(2,1)}, u32[]{:S(2)}, u32[]{:S(2)}) collective-permute-start(bf16[1,8,8,128,128]{4,3,1,2,0:T(8,128)(2,1)} %slice_bitcast_fusion.1), channel_id=1, source_target_pairs={{8,0},{16,8},{24,16},{32,24},{40,32},{48,40},{56,48},{64,56},{72,6... | collective-permute-start | bytes 6291464 | tf_op jit(solution)/shard_map/ppermute | solution.py:15
  170.1 3.5 copy-start.2
  173.6 39.7 %collective-permute-start = (bf16[2,4,8,128,128]{4,3,0,1,2:T(8,128)(2,1)}, bf16[2,4,8,128,128]{4,3,0,1,2:T(8,128)(2,1)}, u32[]{:S(2)}, u32[]{:S(2)}) collective-permute-start(bf16[2,4,8,128,128]{4,3,0,1,2:T(8,128)(2,1)} %get-tuple-element.33), channel_id=1, source_target_pairs={{0,8},{8,16},{16,24},{24,32},{32,40},{40,48},{48,56},{56,64},{64,7... | collective-permute-start | bytes 6291464 | tf_op jit(solution)/shard_map/ppermute | solution.py:12
  177.3 40.5 %collective-permute-start.1 = (bf16[2,4,8,128,128]{4,3,0,1,2:T(8,128)(2,1)}, bf16[2,4,8,128,128]{4,3,0,1,2:T(8,128)(2,1)}, u32[]{:S(2)}, u32[]{:S(2)}) collective-permute-start(bf16[2,4,8,128,128]{4,3,0,1,2:T(8,128)(2,1)} %get-tuple-element.34), channel_id=1, source_target_pairs={{8,0},{16,8},{24,16},{32,24},{40,32},{48,40},{56,48},{64,56},{72,6... | collective-permute-start | bytes 6291464 | tf_op jit(solution)/shard_map/ppermute | solution.py:15
  199.0 12.5 %copy-start.1 = (bf16[1,24,8,128,128]{4,3,1,2,0:T(8,128)(2,1)}, bf16[1,24,8,128,128]{4,3,1,2,0:T(8,128)(2,1)S(1)}, u32[]{:S(2)}) copy-start(bf16[1,24,8,128,128]{4,3,1,2,0:T(8,128)(2,1)S(1)} %pad_maximum_fusion.1) | copy-start | bytes 18874372
  199.0 12.4 %copy-start.3 = (bf16[2,8,8,128,128]{4,3,0,1,2:T(8,128)(2,1)S(1)}, bf16[2,8,8,128,128]{4,3,0,1,2:T(8,128)(2,1)}, u32[]{:S(2)}) copy-start(bf16[2,8,8,128,128]{4,3,0,1,2:T(8,128)(2,1)} %copy-done.2) | copy-start | bytes 12582916
  230.1 3.6 copy-start.12
  233.7 5.2 %collective-permute-start.4 = (s32[4,8]{1,0:T(4,128)S(1)}, s32[4,8]{1,0:T(4,128)S(1)}, u32[]{:S(2)}, u32[]{:S(2)}) collective-permute-start(s32[4,8]{1,0:T(4,128)S(1)} %get-tuple-element.35), channel_id=1, source_target_pairs={{0,8},{8,16},{16,24},{24,32},{32,40},{40,48},{48,56},{56,64},{64,7... | collective-permute-start | bytes 392 | tf_op jit(solution)/shard_map/ppermute | solution.py:12
  235.6 4.9 %collective-permute-start.5 = (s32[4,8]{1,0:T(4,128)S(1)}, s32[4,8]{1,0:T(4,128)S(1)}, u32[]{:S(2)}, u32[]{:S(2)}) collective-permute-start(s32[4,8]{1,0:T(4,128)S(1)} %get-tuple-element.36), channel_id=1, source_target_pairs={{8,0},{16,8},{24,16},{32,24},{40,32},{48,40},{56,48},{64,56},{72,6... | collective-permute-start | bytes 392 | tf_op jit(solution)/shard_map/ppermute | solution.py:15
  240.6 4.2 %copy-start.9 = (bf16[1,16,8,128,128]{4,3,1,2,0:T(8,128)(2,1)S(1)}, bf16[1,16,8,128,128]{4,3,1,2,0:T(8,128)(2,1)}, u32[]{:S(2)}) copy-start(bf16[1,16,8,128,128]{4,3,1,2,0:T(8,128)(2,1)} %get-tuple-element.26) | copy-start | bytes 12582916
  240.6 7.6 %slice-start = ((s8[6291456]{0:T(1024)(128)(4,1)}), s8[4194304]{0:T(1024)(128)(4,1)S(1)}, s32[]{:S(2)}) async-start(s8[6291456]{0:T(1024)(128)(4,1)} %bitcast.467), calls=%async_computation.5 | async-start | bytes 8388608
  244.4 4.9 %slice-start.1 = ((s8[6291456]{0:T(1024)(128)(4,1)}), s8[2097152]{0:T(1024)(128)(4,1)S(1)}, s32[]{:S(2)}) async-start(s8[6291456]{0:T(1024)(128)(4,1)} %bitcast.467), calls=%async_computation.6 | async-start | bytes 4194304
  244.9 4.4 %copy-start.8 = (bf16[1,16,8,128,128]{4,3,1,2,0:T(8,128)(2,1)S(1)}, bf16[1,16,8,128,128]{4,3,1,2,0:T(8,128)(2,1)}, u32[]{:S(2)}) copy-start(bf16[1,16,8,128,128]{4,3,1,2,0:T(8,128)(2,1)} %get-tuple-element.29) | copy-start | bytes 12582916
  267.1 4.5 %copy-start.7 = (bf16[16,8,128,128]{3,2,0,1:T(8,128)(2,1)S(1)}, bf16[16,8,128,128]{3,2,0,1:T(8,128)(2,1)}, u32[]{:S(2)}) copy-start(bf16[16,8,128,128]{3,2,0,1:T(8,128)(2,1)} %get-tuple-element.24) | copy-start | bytes 12582916
  286.0 8.9 %copy-start.5 = (f32[16,128,8,128]{3,1,2,0:T(8,128)S(1)}, f32[16,128,8,128]{3,1,2,0:T(8,128)}, u32[]{:S(2)}) copy-start(f32[16,128,8,128]{3,1,2,0:T(8,128)} %fusion.12) | copy-start | bytes 25165828
  291.1 30.4 %collective-permute-start.6 = (bf16[2,4,8,128,128]{4,3,0,1,2:T(8,128)(2,1)}, bf16[2,4,8,128,128]{4,3,0,1,2:T(8,128)(2,1)S(1)}, u32[]{:S(2)}, u32[]{:S(2)}) collective-permute-start(bf16[2,4,8,128,128]{4,3,0,1,2:T(8,128)(2,1)} %get-tuple-element.32), channel_id=1, source_target_pairs={{0,8},{8,16},{16,24},{24,32},{32,40},{40,48},{48,56},{56,64},{64,7... | collective-permute-start | bytes 6291464 | tf_op jit(solution)/shard_map/ppermute | solution.py:12
  294.9 22.6 %copy-start.4 = (bf16[2,8,1024,128]{3,2,0,1:T(8,128)(2,1)S(1)}, bf16[2,8,1024,128]{3,2,0,1:T(8,128)(2,1)}, u32[]{:S(2)}) copy-start(bf16[2,8,1024,128]{3,2,0,1:T(8,128)(2,1)} %all-gather.3.cloned.1.call-done) | copy-start | bytes 12582916
  315.1 4.9 %copy-start.6 = (bf16[16,128,8,128]{3,1,2,0:T(8,128)(2,1)S(1)}, bf16[16,128,8,128]{3,1,2,0:T(8,128)(2,1)}, u32[]{:S(2)}) copy-start(bf16[16,128,8,128]{3,1,2,0:T(8,128)(2,1)} %select_convert_fusion) | copy-start | bytes 12582916
  315.1 27.8 %collective-permute-start.7 = (bf16[2,4,8,128,128]{4,3,0,1,2:T(8,128)(2,1)}, bf16[2,4,8,128,128]{4,3,0,1,2:T(8,128)(2,1)S(1)}, u32[]{:S(2)}, u32[]{:S(2)}) collective-permute-start(bf16[2,4,8,128,128]{4,3,0,1,2:T(8,128)(2,1)} %get-tuple-element.31), channel_id=1, source_target_pairs={{8,0},{16,8},{24,16},{32,24},{40,32},{48,40},{56,48},{64,56},{72,6... | collective-permute-start | bytes 6291464 | tf_op jit(solution)/shard_map/ppermute | solution.py:15
  344.7 1.0 copy-start.10
  346.2 0.8 copy-start.11
  398.2 12.7 %all-to-all-start.3 = ((f32[32,1,2,96]{3,2,1,0:T(2,128)}), f32[32,1,2,96]{3,2,1,0:T(2,128)S(1)}, u32[]{:S(2)}, u32[]{:S(2)}) async-start(f32[32,1,2,96]{3,2,1,0:T(2,128)} %broadcast_in_dim.170), calls=%async_computation.3 | async-start | bytes 65536 | tf_op jit(solution)/shard_map/all_to_all | solution.py:22
Sparse Core Ops, SparseCore 0:
  233.8 52.1 all-gather.2
